TPU v7x, 32 devices: a whole 2x2x4 slice. The times are simulated.
32 devices in a mesh: dp: 8 (over z, y), inner: 4 (over x, core).
Axes of the slice: x: 2, y: 2, z: 4, core: 2. Of those that a mesh axis runs over, the one named last changes fastest.
Arguments:
- tokens: bfloat16 [32768, 512], P(('dp', 'inner')), may hold values from -6 to 6
- segments: int32 [32768], P(('dp', 'inner')), may hold values from 0 to 32767, as said below
- positions: int32 [32768], P(('dp', 'inner')), may hold values from 0 to 1023, as said below
- cotangent: bfloat16 [32768, 512], P(('dp', 'inner')), may hold values from -6 to 6
- attn_weight: float32 [4, 512, 512], P(None, ('dp', 'inner')), may hold values from -0.53033009 to 0.53033009
- attn_m: float32 [4, 512, 512], P(None, ('dp', 'inner')), may hold values from -0.0007324219 to 0.0007324219
- attn_v: float32 [4, 512, 512], P(None, ('dp', 'inner')), may hold values from 1.0882435e-09 to 4.352974e-09
- gate_weight: float32 [2, 512, 512], P(None, ('dp', 'inner')), may hold values from -0.25 to 0.25
- gate_m: float32 [2, 512, 512], P(None, ('dp', 'inner')), may hold values from -0.00036621094 to 0.00036621094
- gate_v: float32 [2, 512, 512], P(None, ('dp', 'inner')), may hold values from 2.7206087e-10 to 1.0882435e-09
- in_weight: float32 [512, 2048], P(('dp', 'inner')), may hold values from -0.25 to 0.25
- in_m: float32 [512, 2048], P(('dp', 'inner')), may hold values from -0.00036621094 to 0.00036621094
- in_v: float32 [512, 2048], P(('dp', 'inner')), may hold values from 2.7206087e-10 to 1.0882435e-09
- out_weight: float32 [2048, 512], P(('dp', 'inner')), may hold values from -0.125 to 0.125
- out_m: float32 [2048, 512], P(('dp', 'inner')), may hold values from -0.00036621094 to 0.00036621094
- out_v: float32 [2048, 512], P(('dp', 'inner')), may hold values from 2.7206087e-10 to 1.0882435e-09
- norm_params: float32 [7, 512], P(None, ('dp', 'inner'))
- norm_m: float32 [7, 512], P(None, ('dp', 'inner')), may hold values from -0.0014648438 to 0.0014648438
- norm_v: float32 [7, 512], P(None, ('dp', 'inner')), may hold values from 4.352974e-09 to 1.7411896e-08
- in_bias: float32 [2048], P(('dp', 'inner')), may hold values from -1.75 to 1.75
- bias_m: float32 [2048], P(('dp', 'inner')), may hold values from -0.00024414062 to 0.00024414062
- bias_v: float32 [2048], P(('dp', 'inner')), may hold values from 1.7411896e-10 to 7.073583e-10
Outputs:
- layer_out: bfloat16 [32768, 512], P(('dp', 'inner'))
- input_grad: bfloat16 [32768, 512], P(('dp', 'inner'))
- grad_norm: float32 [], replicated
- attn_new: float32 [4, 512, 512], P(None, ('dp', 'inner'))
- attn_m_new: float32 [4, 512, 512], P(None, ('dp', 'inner'))
- attn_v_new: float32 [4, 512, 512], P(None, ('dp', 'inner'))
- gate_new: float32 [2, 512, 512], P(None, ('dp', 'inner'))
- gate_m_new: float32 [2, 512, 512], P(None, ('dp', 'inner'))
- gate_v_new: float32 [2, 512, 512], P(None, ('dp', 'inner'))
- in_new: float32 [512, 2048], P(('dp', 'inner'))
- in_m_new: float32 [512, 2048], P(('dp', 'inner'))
- in_v_new: float32 [512, 2048], P(('dp', 'inner'))
- out_new: float32 [2048, 512], P(('dp', 'inner'))
- out_m_new: float32 [2048, 512], P(('dp', 'inner'))
- out_v_new: float32 [2048, 512], P(('dp', 'inner'))
- norm_new: float32 [7, 512], P(None, ('dp', 'inner'))
- norm_m_new: float32 [7, 512], P(None, ('dp', 'inner'))
- norm_v_new: float32 [7, 512], P(None, ('dp', 'inner'))
- bias_new: float32 [2048], P(('dp', 'inner'))
- bias_m_new: float32 [2048], P(('dp', 'inner'))
- bias_v_new: float32 [2048], P(('dp', 'inner'))
Inputs may be any that keep to these rules, and one draw needn't show every extreme that they name: `segments`: a token's segment number is the index of its document's first token, so segment numbers never fall; a new document begins at every sequence start (every 1024 tokens); the first sequence is one document; the last token forms a document of its own. positions restart at 0 with every new segment number.
All inputs are finite; a program needn't handle non-finite values.
Results may differ from a plain program's by a relative error of at most 0.033.
The roundings to bfloat16 on the way count: a program that leaves them out, or rounds other values in their place, can miss the bound.
Values may be sent and summed in bfloat16 or wider, within the bound.
No kernel may reach another device: no remote copies, remote signals or barrier semaphores. Data moves between devices by JAX's collectives and lax.ppermute only.
A program may use at most 192 MiB of HBM per device.

v0:
```python
import jax
import jax.numpy as jnp
from jax import lax
from jax.sharding import PartitionSpec as P

HEADS = 8
HEAD = 64
STEP = 10


norm_eps = 1e-05
first_decay = 0.9
second_decay = 0.999
adam_eps = 1e-08
learn_rate = 0.05
vector_rate = 0.8
weight_decay = 0.1
clip_norm = 1.0
masked_score = -1e30


def normalize_parts(values, gain_row, bias_row):
    centred = values - jnp.mean(values, -1, keepdims=True)
    spread = jnp.mean(centred * centred, -1, keepdims=True)
    scale_row = lax.rsqrt(spread + norm_eps)
    unit_rows = centred * scale_row
    return (unit_rows * gain_row + bias_row, unit_rows, scale_row)


def normalize_back(grad_rows, unit_rows, scale_row, gain_row):
    grad_unit = grad_rows * gain_row
    return scale_row * (
        grad_unit
        - jnp.mean(grad_unit, -1, keepdims=True)
        - unit_rows * jnp.mean(grad_unit * unit_rows, -1, keepdims=True)
    )


def fetch(shards):
    low_attn, low_gate, low_in, low_out, low_vec, low_shift = [
        element.astype(jnp.bfloat16) for element in shards
    ]
    return (
        lax.all_gather(low_attn, ("dp", "inner"), axis=1, tiled=True),
        lax.all_gather(low_gate, ("dp", "inner"), axis=1, tiled=True),
        lax.all_gather(low_in, ("dp", "inner"), axis=0, tiled=True),
        lax.all_gather(low_out, ("dp", "inner"), axis=0, tiled=True),
        lax.all_gather(low_vec, ("dp", "inner"), axis=1, tiled=True),
        lax.all_gather(low_shift, ("dp", "inner"), axis=0, tiled=True),
    )


def score_block(queries, key_heads, segments, positions, first_row, block_size):
    query_part = lax.slice_in_dim(queries, first_row, first_row + block_size, axis=0)
    raw_scores = jnp.einsum(
        "qhe,khe->hqk", query_part, key_heads, preferred_element_type=jnp.float32
    )
    own_segments = lax.slice_in_dim(segments, first_row, first_row + block_size, axis=0)
    own_positions = lax.slice_in_dim(positions, first_row, first_row + block_size, axis=0)
    allowed = (own_segments[:, None] == segments[None, :]) & (
        positions[None, :] <= own_positions[:, None]
    )
    return (jnp.where(allowed[None], raw_scores * HEAD ** (-0.5), masked_score), query_part)


def attend(triple, segments, positions):
    row_count = triple.shape[1]
    block_size = min(512, row_count)
    queries = triple[0].reshape(row_count, HEADS, HEAD)
    key_heads = triple[1].reshape(row_count, HEADS, HEAD)
    value_heads = triple[2].reshape(row_count, HEADS, HEAD)
    mixed_parts = []
    total_parts = []
    for first_row in range(0, row_count, block_size):
        scores, query_part = score_block(
            queries, key_heads, segments, positions, first_row, block_size
        )
        row_max = jnp.max(scores, -1, keepdims=True)
        weights = jnp.exp(scores - row_max)
        exp_total = jnp.sum(weights, -1, keepdims=True)
        attn_probs = (weights / exp_total).astype(jnp.bfloat16)
        mixed_block = jnp.einsum(
            "hqk,khe->qhe", attn_probs, value_heads, preferred_element_type=jnp.float32
        )
        mixed_parts.append(mixed_block.reshape(block_size, HEADS * HEAD))
        total_parts.append(row_max + jnp.log(exp_total))
    mixed_heads = jnp.concatenate(mixed_parts, 0).astype(jnp.bfloat16)
    return (mixed_heads, jnp.concatenate(total_parts, 1))


def attend_back(triple, grad_mixed, log_total, segments, positions):
    row_count = triple.shape[1]
    block_size = min(512, row_count)
    queries = triple[0].reshape(row_count, HEADS, HEAD)
    key_heads = triple[1].reshape(row_count, HEADS, HEAD)
    value_heads = triple[2].reshape(row_count, HEADS, HEAD)
    grad_heads = grad_mixed.reshape(row_count, HEADS, HEAD)
    query_grads = []
    grad_keys = jnp.zeros((row_count, HEADS, HEAD), jnp.float32)
    grad_values = jnp.zeros((row_count, HEADS, HEAD), jnp.float32)
    for first_row in range(0, row_count, block_size):
        scores, query_part = score_block(
            queries, key_heads, segments, positions, first_row, block_size
        )
        attn_probs = jnp.exp(
            scores - lax.slice_in_dim(log_total, first_row, first_row + block_size, axis=1)
        )
        grad_part = lax.slice_in_dim(grad_heads, first_row, first_row + block_size, axis=0)
        grad_probs = jnp.einsum(
            "qhe,khe->hqk", grad_part, value_heads, preferred_element_type=jnp.float32
        )
        row_inner = jnp.sum(attn_probs * grad_probs, -1, keepdims=True)
        grad_raw = (attn_probs * (grad_probs - row_inner) * HEAD ** (-0.5)).astype(jnp.bfloat16)
        query_grads.append(
            jnp.einsum(
                "hqk,khe->qhe", grad_raw, key_heads, preferred_element_type=jnp.float32
            ).reshape(block_size, HEADS * HEAD)
        )
        grad_keys = grad_keys + jnp.einsum(
            "hqk,qhe->khe", grad_raw, query_part, preferred_element_type=jnp.float32
        )
        grad_values = grad_values + jnp.einsum(
            "hqk,qhe->khe",
            attn_probs.astype(jnp.bfloat16),
            grad_part,
            preferred_element_type=jnp.float32,
        )
    grad_query_rows = jnp.concatenate(query_grads, 0)
    stacked = jnp.stack(
        [
            grad_query_rows,
            grad_keys.reshape(row_count, HEADS * HEAD),
            grad_values.reshape(row_count, HEADS * HEAD),
        ]
    )
    return stacked.astype(jnp.bfloat16)


def attn_branch(weights, normed, segments, positions):
    triple = jnp.einsum(
        "td,jde->jte", normed, weights[0][:3], preferred_element_type=jnp.float32
    ).astype(jnp.bfloat16)
    mixed_heads, log_total = attend(triple, segments, positions)
    attended = jnp.dot(mixed_heads, weights[0][3], preferred_element_type=jnp.float32)
    return (triple, mixed_heads, log_total, attended)


def ffn_branch(weights, normed_two):
    hidden = jnp.dot(normed_two, weights[2], preferred_element_type=jnp.float32) + weights[
        5
    ].astype(jnp.float32)
    active = jnp.maximum(hidden, 0.0).astype(jnp.bfloat16)
    branch = jnp.dot(active, weights[3], preferred_element_type=jnp.float32) + weights[4][6].astype(
        jnp.float32
    )
    return (hidden, active, branch)


def adam_update(weight, first_moment, second_moment, gradient, factor, step_rate):
    clipped = gradient * factor
    first_new = first_decay * first_moment + (1.0 - first_decay) * clipped
    second_new = second_decay * second_moment + (1.0 - second_decay) * clipped * clipped
    corrected = first_new / (1.0 - first_decay**STEP)
    spread = second_new / (1.0 - second_decay**STEP)
    weight_new = weight - step_rate * (
        corrected / (jnp.sqrt(spread) + adam_eps) + weight_decay * weight
    )
    return (weight_new, first_new, second_new)


def body(
    tokens,
    segments,
    positions,
    cotangent,
    attn_weight,
    attn_m,
    attn_v,
    gate_weight,
    gate_m,
    gate_v,
    in_weight,
    in_m,
    in_v,
    out_weight,
    out_m,
    out_v,
    norm_params,
    norm_m,
    norm_v,
    in_bias,
    bias_m,
    bias_v,
):
    shards = (attn_weight, gate_weight, in_weight, out_weight, norm_params, in_bias)
    weights = fetch(shards)
    vectors = weights[4].astype(jnp.float32)
    inputs = tokens.astype(jnp.float32)
    normed_full, unit_one, scale_one = normalize_parts(inputs, vectors[0], vectors[1])
    normed = normed_full.astype(jnp.bfloat16)
    triple, mixed_heads, log_total, attended = attn_branch(weights, normed, segments, positions)
    attn_gate = jax.nn.sigmoid(
        jnp.dot(normed, weights[1][0], preferred_element_type=jnp.float32) + vectors[4]
    )
    middle = attn_gate * attended + (1.0 - attn_gate) * inputs
    normed_two_full, unit_two, scale_two = normalize_parts(middle, vectors[2], vectors[3])
    normed_two = normed_two_full.astype(jnp.bfloat16)
    hidden, active, branch = ffn_branch(weights, normed_two)
    ffn_gate = jax.nn.sigmoid(
        jnp.dot(normed_two, weights[1][1], preferred_element_type=jnp.float32) + vectors[5]
    )
    layer_out = (ffn_gate * branch + (1.0 - ffn_gate) * middle).astype(jnp.bfloat16)
    weights = fetch(shards)
    triple, mixed_heads, log_total, attended = attn_branch(weights, normed, segments, positions)
    hidden, active, branch = ffn_branch(weights, normed_two)
    grad_out = cotangent.astype(jnp.float32)
    grad_branch = grad_out * ffn_gate
    grad_fgate = grad_out * (branch - middle) * ffn_gate * (1.0 - ffn_gate)
    grad_middle = grad_out * (1.0 - ffn_gate)
    branch_low = grad_branch.astype(jnp.bfloat16)
    grad_w_out = jnp.einsum("tf,td->fd", active, branch_low, preferred_element_type=jnp.float32)
    grad_active = jnp.einsum(
        "td,fd->tf", branch_low, weights[3], preferred_element_type=jnp.float32
    )
    grad_hidden = jnp.where(hidden > 0.0, grad_active, 0.0)
    hidden_low = grad_hidden.astype(jnp.bfloat16)
    grad_w_in = jnp.einsum("td,tf->df", normed_two, hidden_low, preferred_element_type=jnp.float32)
    fgate_low = grad_fgate.astype(jnp.bfloat16)
    grad_w_fgate = jnp.einsum(
        "td,te->de", normed_two, fgate_low, preferred_element_type=jnp.float32
    )
    grad_normed_two = jnp.einsum(
        "tf,df->td", hidden_low, weights[2], preferred_element_type=jnp.float32
    )
    grad_normed_two = grad_normed_two + jnp.einsum(
        "te,de->td", fgate_low, weights[1][1], preferred_element_type=jnp.float32
    )
    grad_gain_two = jnp.sum(grad_normed_two * unit_two, 0)
    grad_shift_two = jnp.sum(grad_normed_two, 0)
    grad_middle = grad_middle + normalize_back(grad_normed_two, unit_two, scale_two, vectors[2])
    grad_attended = grad_middle * attn_gate
    grad_agate = grad_middle * (attended - inputs) * attn_gate * (1.0 - attn_gate)
    grad_inputs = grad_middle * (1.0 - attn_gate)
    attended_low = grad_attended.astype(jnp.bfloat16)
    grad_w_o = jnp.einsum(
        "td,te->de", mixed_heads, attended_low, preferred_element_type=jnp.float32
    )
    grad_mixed = jnp.einsum(
        "te,de->td", attended_low, weights[0][3], preferred_element_type=jnp.float32
    ).astype(jnp.bfloat16)
    triple_grad = attend_back(triple, grad_mixed, log_total, segments, positions)
    grad_w_qkv = jnp.einsum("td,jte->jde", normed, triple_grad, preferred_element_type=jnp.float32)
    agate_low = grad_agate.astype(jnp.bfloat16)
    grad_w_agate = jnp.einsum("td,te->de", normed, agate_low, preferred_element_type=jnp.float32)
    grad_normed = jnp.einsum(
        "jte,jde->td", triple_grad, weights[0][:3], preferred_element_type=jnp.float32
    )
    grad_normed = grad_normed + jnp.einsum(
        "te,de->td", agate_low, weights[1][0], preferred_element_type=jnp.float32
    )
    grad_gain_one = jnp.sum(grad_normed * unit_one, 0)
    grad_shift_one = jnp.sum(grad_normed, 0)
    grad_inputs = grad_inputs + normalize_back(grad_normed, unit_one, scale_one, vectors[0])
    input_grad = grad_inputs.astype(jnp.bfloat16)
    grad_attn = jnp.concatenate([grad_w_qkv, grad_w_o[None]], 0)
    grad_gates = jnp.stack([grad_w_agate, grad_w_fgate])
    grad_vectors = jnp.stack(
        [
            grad_gain_one,
            grad_shift_one,
            grad_gain_two,
            grad_shift_two,
            jnp.sum(grad_agate, 0),
            jnp.sum(grad_fgate, 0),
            jnp.sum(grad_branch, 0),
        ]
    )
    grad_bias = jnp.sum(grad_hidden, 0)
    owned = (
        lax.psum_scatter(grad_attn, ("dp", "inner"), scatter_dimension=1, tiled=True),
        lax.psum_scatter(grad_gates, ("dp", "inner"), scatter_dimension=1, tiled=True),
        lax.psum_scatter(grad_w_in, ("dp", "inner"), scatter_dimension=0, tiled=True),
        lax.psum_scatter(grad_w_out, ("dp", "inner"), scatter_dimension=0, tiled=True),
        lax.psum_scatter(grad_vectors, ("dp", "inner"), scatter_dimension=1, tiled=True),
        lax.psum_scatter(grad_bias, ("dp", "inner"), scatter_dimension=0, tiled=True),
    )
    local_squares = sum((jnp.sum(element * element) for element in owned))
    grad_norm = jnp.sqrt(lax.psum(local_squares, ("dp", "inner")))
    factor = jnp.minimum(1.0, clip_norm / (grad_norm + 1e-06))
    states = (
        (attn_weight, attn_m, attn_v),
        (gate_weight, gate_m, gate_v),
        (in_weight, in_m, in_v),
        (out_weight, out_m, out_v),
        (norm_params, norm_m, norm_v),
        (in_bias, bias_m, bias_v),
    )
    step_rates = (learn_rate, learn_rate, learn_rate, learn_rate, vector_rate, vector_rate)
    updated = [
        adam_update(state[0], state[1], state[2], gradient, factor, step_rate)
        for state, gradient, step_rate in zip(states, owned, step_rates)
    ]
    return (
        layer_out,
        input_grad,
        grad_norm,
        updated[0][0],
        updated[0][1],
        updated[0][2],
        updated[1][0],
        updated[1][1],
        updated[1][2],
        updated[2][0],
        updated[2][1],
        updated[2][2],
        updated[3][0],
        updated[3][1],
        updated[3][2],
        updated[4][0],
        updated[4][1],
        updated[4][2],
        updated[5][0],
        updated[5][1],
        updated[5][2],
    )


def solution(mesh):
    return jax.shard_map(
        body,
        mesh=mesh,
        in_specs=(
            P(("dp", "inner"), None),
            P(("dp", "inner")),
            P(("dp", "inner")),
            P(("dp", "inner"), None),
            P(None, ("dp", "inner"), None),
            P(None, ("dp", "inner"), None),
            P(None, ("dp", "inner"), None),
            P(None, ("dp", "inner"), None),
            P(None, ("dp", "inner"), None),
            P(None, ("dp", "inner"), None),
            P(("dp", "inner"), None),
            P(("dp", "inner"), None),
            P(("dp", "inner"), None),
            P(("dp", "inner"), None),
            P(("dp", "inner"), None),
            P(("dp", "inner"), None),
            P(None, ("dp", "inner")),
            P(None, ("dp", "inner")),
            P(None, ("dp", "inner")),
            P(("dp", "inner")),
            P(("dp", "inner")),
            P(("dp", "inner")),
        ),
        out_specs=(
            P(("dp", "inner"), None),
            P(("dp", "inner"), None),
            P(),
            P(None, ("dp", "inner"), None),
            P(None, ("dp", "inner"), None),
            P(None, ("dp", "inner"), None),
            P(None, ("dp", "inner"), None),
            P(None, ("dp", "inner"), None),
            P(None, ("dp", "inner"), None),
            P(("dp", "inner"), None),
            P(("dp", "inner"), None),
            P(("dp", "inner"), None),
            P(("dp", "inner"), None),
            P(("dp", "inner"), None),
            P(("dp", "inner"), None),
            P(None, ("dp", "inner")),
            P(None, ("dp", "inner")),
            P(None, ("dp", "inner")),
            P(("dp", "inner")),
            P(("dp", "inner")),
            P(("dp", "inner")),
        ),
        check_vma=False,
    )
```

profile of v0, /device:TPU:0, one launch (start us, length us, event | category | flops | bytes accessed | tf_op | source)
XLA Modules:
  0.0 1209.7 jit_solution(3663491869928504730)
XLA Ops:
  7.3 1.7 copy.146
  9.0 1.5 convert_element_type.108
  10.6 1.5 convert_element_type.115
  12.2 1.5 convert_element_type.119
  15.2 1.4 convert_reduce_fusion
  17.4 42.1 %all-reduce = bf16[2048]{0:T(1024)(128)(2,1)S(1)} all-reduce(bf16[2048]{0:T(1024)(128)(2,1)S(1)} %dynamic-update-slice), channel_id=1, replica_groups=mesh['dp'=8,'inner'=4] {'dp','inner'}, use_global_device_ids=true, to_apply=%add | all-reduce | flops 2048 | bytes 8192
  59.6 40.4 %all-gather = bf16[32,16,7]{1,2,0:T(8,128)(2,1)S(1)} all-gather(bf16[1,16,7]{1,2,0:T(8,128)(2,1)S(1)} %convert_bitcast_fusion.1), channel_id=1, replica_groups=mesh['dp'=8,'inner'=4] {'dp','inner'}, dimensions={0}, use_global_device_ids=true | all-gather | bytes 7392 | tf_op jit(solution)/shard_map/all_gather | solution.py:48
  101.6 4.1 copy.135
  105.7 3.4 convert_bitcast_fusion
  110.0 3.2 fusion.139
  113.2 3.5 fusion.9
  116.7 2.2 copy-done
  118.9 3.8 fusion.82
  122.8 3.2 fusion.140
  126.0 4.1 fusion.8
  132.3 3.8 fusion.83
  136.9 2.1 fusion.89
  139.0 5.1 fusion.131
  144.6 40.8 %all-gather.10.cloned.1.call-done = bf16[512,2048]{1,0:T(8,128)(2,1)} async-done(((bf16[16,2048]{1,0:T(8,128)(2,1)}), bf16[512,2048]{1,0:T(8,128)(2,1)}) %all-gather.10.cloned.1.call-update) | async-done | bytes 2097168 | tf_op jit(solution)/shard_map/all_gather | solution.py:46
  185.4 7.2 fusion.142
  192.6 51.2 %all-gather.12.cloned.1.call-done = bf16[2048,512]{1,0:T(8,128)(2,1)} async-done(((bf16[64,512]{1,0:T(8,128)(2,1)}), bf16[2048,512]{1,0:T(8,128)(2,1)}) %all-gather.12.cloned.1.call-update) | async-done | bytes 2097168 | tf_op jit(solution)/shard_map/all_gather | solution.py:47
  243.7 6.5 fusion.86
  250.2 3.2 fusion.126
  253.4 3.0 fusion.141
  256.4 2.4 fusion.68
  258.9 1.4 multiply_reduce_fusion.2
  261.4 2.3 fusion.128
  265.6 1.8 convolution_bitcast_fusion.3
  269.8 8.1 fusion.143
  277.9 29.8 %fusion.79 = bf16[8,64,512]{2,1,0:T(8,128)(2,1)} fusion(bf16[1024,8,64]{0,2,1:T(8,128)(2,1)} %bitcast.126, f32[8,512,1024]{2,1,0:T(8,128)} %fusion.143, f32[8,512,1024]{2,1,0:T(8,128)} %copy-done.1, f32[8,512]{1,0:T(8,128)S(1)} %log_add_fusion.1), kind=kOutput, calls=%fused_computation.102 | convolution fusion | flops 566498304 | bytes 35143680 | tf_op jit(solution)/shard_map/hqk,khe->qhe/dot_general | solution.py:115
  307.7 31.1 %fusion.13 = f32[8,64,1024]{2,1,0:T(8,128)} fusion(bf16[512,8,64]{0,2,1:T(8,128)(2,1)} %bitcast.137, f32[8,512,1024]{2,1,0:T(8,128)} %fusion.143, f32[8,512,1024]{2,1,0:T(8,128)} %copy-done.1, f32[8,512]{1,0:T(8,128)S(1)} %log_add_fusion.1), kind=kOutput, calls=%fused_computation.20 | convolution fusion | flops 566236160 | bytes 36192256 | tf_op jit(solution)/shard_map/hqk,qhe->khe/dot_general | solution.py:119
  338.8 9.5 fusion.144
  348.4 7.4 fusion.24
  355.8 3.9 add_convert_fusion
  359.7 2.4 copy.124
  362.1 2.1 copy.121
  364.1 37.1 %fusion.76 = bf16[8,64,512]{2,1,0:T(8,128)(2,1)} fusion(bf16[1024,8,64]{0,2,1:T(8,128)(2,1)S(1)} %bitcast.127, f32[8,512,1024]{2,1,0:T(8,128)} %fusion.144, f32[8,512,1024]{2,1,0:T(8,128)} %copy-done, f32[8,512]{1,0:T(8,128)S(1)} %log_add_fusion), kind=kOutput, calls=%fused_computation.101 | convolution fusion | flops 566498304 | bytes 35143680 | tf_op jit(solution)/shard_map/hqk,khe->qhe/dot_general | solution.py:115
  401.2 31.8 %add_convert_fusion.1 = bf16[8,64,1024]{2,1,0:T(8,128)(2,1)} fusion(f32[8,64,1024]{2,1,0:T(8,128)} %fusion.13, bf16[512,8,64]{0,2,1:T(8,128)(2,1)} %bitcast.135, f32[8,512,1024]{2,1,0:T(8,128)} %fusion.144, f32[8,512,1024]{2,1,0:T(8,128)} %copy-done, f32[8,512]{1,0:T(8,128)S(1)} %log_add_fusion), kind=kOutput, calls=%fused_computation.76 | convolution fusion | flops 567284736 | bytes 37240832 | tf_op jit(solution)/shard_map/hqk,qhe->khe/dot_general | solution.py:119
  434.4 2.3 copy.123
  438.1 3.5 fusion.84
  441.6 3.7 convolution_bitcast_fusion
  445.3 2.6 fusion.57
  448.9 4.6 pad_maximum_fusion
  453.5 5.4 copy.128
  459.0 2.4 convolution_bitcast_fusion.2
  462.6 1.5 pad_maximum_fusion.2
  464.3 6.7 fusion.66
  471.1 1.5 copy-done.16
  472.6 8.0 fusion.85
  480.6 38.5 %all-reduce.2 = f32[2048]{0:T(1024)S(1)} all-reduce(f32[2048]{0:T(1024)S(1)} %get-tuple-element.168), channel_id=7, replica_groups=mesh['dp'=8,'inner'=4] {'dp','inner'}, use_global_device_ids=true, to_apply=%region_32.33.clone | all-reduce | flops 2048 | bytes 16384
  520.3 63.1 %reduce-scatter.13.cloned.1.call-done = f32[16,7]{1,0:T(8,128)} async-done(((f32[512,7]{1,0:T(8,128)}), f32[16,7]{1,0:T(8,128)}) %reduce-scatter.13.cloned.1.call-update) | async-done | bytes 464
  584.8 142.4 %all-reduce.5.cloned.1.call-done = f32[4,512,512]{2,0,1:T(4,128)} async-done(((f32[4,512,512]{2,0,1:T(4,128)}), f32[4,512,512]{2,0,1:T(4,128)}) %all-reduce.5.cloned.1.call-update) | async-done | bytes 4194320
  727.2 2.2 multiply_reduce_fusion.9
  729.4 137.4 %reduce-scatter.7.cloned.1.call-done = f32[2,16,512]{2,1,0:T(8,128)} async-done(((f32[2,512,512]{2,1,0:T(8,128)}), f32[2,16,512]{2,1,0:T(8,128)}) %reduce-scatter.7.cloned.1.call-update) | async-done | bytes 65552 | tf_op jit(solution)/shard_map/reduce_scatter | solution.py:281
  866.9 1.5 multiply_reduce_fusion.10
  869.6 137.9 %reduce-scatter.9.cloned.1.call-done = f32[16,2048]{1,0:T(8,128)} async-done(((f32[512,2048]{1,0:T(8,128)}), f32[16,2048]{1,0:T(8,128)}) %reduce-scatter.9.cloned.1.call-update) | async-done | bytes 131088 | tf_op jit(solution)/shard_map/reduce_scatter | solution.py:282
  1007.5 1.5 multiply_reduce_fusion.8
  1009.7 138.5 %reduce-scatter.11.cloned.1.call-done = f32[64,512]{1,0:T(8,128)} async-done(((f32[2048,512]{1,0:T(8,128)}), f32[64,512]{1,0:T(8,128)}) %reduce-scatter.11.cloned.1.call-update) | async-done | bytes 131088 | tf_op jit(solution)/shard_map/reduce_scatter | solution.py:283
  1148.2 1.5 multiply_reduce_fusion.7
  1151.8 3.7 fusion.56
  1155.5 36.9 %psum.7 = f32[]{:T(128)} all-reduce(f32[]{:T(128)S(6)} %add.297), channel_id=1, replica_groups=mesh['dp'=8,'inner'=4] {'dp','inner'}, use_global_device_ids=true, to_apply=%region_34.35 | all-reduce | flops 1 | bytes 8 | tf_op jit(solution)/shard_map/psum | solution.py:288
  1195.7 1.9 multiply_subtract_fusion.2
  1197.6 1.6 multiply_subtract_fusion.3
  1199.2 1.8 multiply_subtract_fusion
  (171 shorter events, 25.1 us)
Async XLA Ops:
  7.2 9.4 copy-start.5
  7.2 93.0 %copy-start.39 = (s32[1024]{0:T(1024)S(1)}, s32[1024]{0:T(1024)}, u32[]{:S(2)}) copy-start(s32[1024]{0:T(1024)} %param.24) | copy-start | bytes 12292
  7.2 93.0 %copy-start.40 = (s32[1024]{0:T(1024)S(1)}, s32[1024]{0:T(1024)}, u32[]{:S(2)}) copy-start(s32[1024]{0:T(1024)} %param.23) | copy-start | bytes 12292
  7.2 94.3 %all-gather.8.cloned.1.call-start = ((), (), s32[]{:S(2)}) async-start(), calls=%async_computation.5 | async-start | bytes 2162688 | tf_op jit(solution)/shard_map/all_gather | solution.py:44
  9.0 130.0 %all-gather.6.cloned.1.call-start = ((), (), s32[]{:S(2)}) async-start(), calls=%async_computation.4 | async-start | bytes 1081344 | tf_op jit(solution)/shard_map/all_gather | solution.py:45
  10.5 174.8 %all-gather.10.cloned.1.call-start = ((), (), s32[]{:S(2)}) async-start(), calls=%async_computation.6 | async-start | bytes 2162688 | tf_op jit(solution)/shard_map/all_gather | solution.py:46
  12.1 231.6 %all-gather.12.cloned.1.call-start = ((), (), s32[]{:S(2)}) async-start(), calls=%async_computation.7 | async-start | bytes 2162688 | tf_op jit(solution)/shard_map/all_gather | solution.py:47
  13.8 569.7 %reduce-scatter.13.cloned.1.call-start = ((), (), s32[]{:S(2)}) async-start(), calls=%async_computation.11 | async-start | bytes 270336
  100.2 358.8 %copy-start.42 = (f32[1,512]{1,0:T(1,128)}, f32[1,512]{1,0:T(1,128)S(1)}, u32[]{:S(2)}) copy-start(f32[1,512]{1,0:T(1,128)S(1)} %get-tuple-element.153) | copy-start | bytes 6148
  109.2 0.8 copy-start.18
  109.2 13.6 %copy-start.19 = (bf16[1,512,512]{1,2,0:T(8,128)(2,1)}, bf16[1,512,512]{1,2,0:T(8,128)(2,1)S(1)}, u32[]{:S(2)}) copy-start(bf16[1,512,512]{1,2,0:T(8,128)(2,1)S(1)} %get-tuple-element.142) | copy-start | bytes 1572868
  109.4 13.4 %copy-start.9 = (bf16[1,1024,512]{1,2,0:T(8,128)(2,1)}, bf16[1,1024,512]{1,2,0:T(8,128)(2,1)S(1)}, u32[]{:S(2)}) copy-start(bf16[1,1024,512]{1,2,0:T(8,128)(2,1)S(1)} %get-tuple-element.144) | copy-start | bytes 3145732
  113.2 5.7 copy-start
  122.7 13.4 %copy-start.45 = (bf16[8,64,512]{2,1,0:T(8,128)(2,1)}, bf16[8,64,512]{2,1,0:T(8,128)(2,1)S(1)}, u32[]{:S(2)}) copy-start(bf16[8,64,512]{2,1,0:T(8,128)(2,1)S(1)} %fusion.82) | copy-start | bytes 1572868
  126.0 6.3 copy-start.1
  126.0 4.1 copy-start.14
  132.3 3.9 copy-start.26
  136.1 0.8 copy-start.47
  243.7 6.5 copy-start.22
  243.7 6.5 copy-start.35
  243.7 9.7 slice-start.4
  250.2 3.2 copy-start.44
  250.2 3.2 slice-start.5
  253.4 5.4 copy-start.23
  253.4 6.8 copy-start.15
  253.4 3.0 copy-start.43
  256.4 2.4 copy-start.8
  258.8 1.6 copy-start.2
  258.8 1.8 copy-start.6
  258.8 2.5 copy-start.17
  263.7 1.3 copy-start.4
  263.7 1.4 copy-start.46
  263.7 2.0 copy-start.48
  265.6 1.8 copy-start.27
  269.0 0.8 copy-start.11
  338.8 9.6 copy-start.13
  338.8 17.0 %slice-start = ((s8[16777216]{0:T(1024)(128)(4,1)}), s8[4194304]{0:T(1024)(128)(4,1)S(1)}, s32[]{:S(2)}) async-start(s8[16777216]{0:T(1024)(128)(4,1)} %bitcast.118), calls=%async_computation.13 | async-start | bytes 8388608
  338.8 17.0 %slice-start.1 = ((s8[16777216]{0:T(1024)(128)(4,1)}), s8[4194304]{0:T(1024)(128)(4,1)S(1)}, s32[]{:S(2)}) async-start(s8[16777216]{0:T(1024)(128)(4,1)} %bitcast.118), calls=%async_computation.14 | async-start | bytes 8388608
  338.8 17.0 %slice-start.2 = ((s8[16777216]{0:T(1024)(128)(4,1)}), s8[4194304]{0:T(1024)(128)(4,1)S(1)}, s32[]{:S(2)}) async-start(s8[16777216]{0:T(1024)(128)(4,1)} %bitcast.118), calls=%async_computation.15 | async-start | bytes 8388608
  348.4 7.5 slice-start.3
  348.4 7.5 copy-start.12
  359.7 4.4 copy-start.10
  433.1 3.6 copy-start.20
  436.7 1.4 copy-start.21
  438.1 3.5 copy-start.7
  438.1 3.5 copy-start.28
  438.1 3.5 copy-start.29
  441.6 3.7 copy-start.25
  441.6 3.7 copy-start.36
  448.8 278.4 %all-reduce.5.cloned.1.call-start = ((), (), s32[]{:S(2)}) async-start(), calls=%async_computation.12 | async-start | bytes 8388608
  458.9 407.9 %reduce-scatter.7.cloned.1.call-start = ((), (), s32[]{:S(2)}) async-start(), calls=%async_computation.8 | async-start | bytes 2162688 | tf_op jit(solution)/shard_map/reduce_scatter | solution.py:281
  459.0 2.4 copy-start.24
  464.1 543.5 %reduce-scatter.9.cloned.1.call-start = ((), (), s32[]{:S(2)}) async-start(), calls=%async_computation.9 | async-start | bytes 4325376 | tf_op jit(solution)/shard_map/reduce_scatter | solution.py:282
  471.0 1.6 copy-start.16
  471.0 677.2 %reduce-scatter.11.cloned.1.call-start = ((), (), s32[]{:S(2)}) async-start(), calls=%async_computation.10 | async-start | bytes 4325376 | tf_op jit(solution)/shard_map/reduce_scatter | solution.py:283
  480.5 671.2 %copy-start.3 = (f32[1024,512]{1,0:T(8,128)S(1)}, f32[1024,512]{1,0:T(8,128)}, u32[]{:S(2)}) copy-start(f32[1024,512]{1,0:T(8,128)} %get-tuple-element.164) | copy-start | bytes 6291460
  519.1 632.7 %copy-start.41 = (f32[2048]{0:T(1024)}, f32[2048]{0:T(1024)S(1)}, u32[]{:S(2)}) copy-start(f32[2048]{0:T(1024)S(1)} %all-reduce.2) | copy-start | bytes 24580
  1151.7 44.0 %copy-start.30 = (f32[4,16,512]{2,1,0:T(8,128)S(1)}, f32[4,16,512]{2,1,0:T(8,128)}, u32[]{:S(2)}) copy-start(f32[4,16,512]{2,1,0:T(8,128)} %param.26) | copy-start | bytes 393220
  1151.8 47.5 %copy-start.31 = (f32[64,512]{1,0:T(8,128)S(1)}, f32[64,512]{1,0:T(8,128)}, u32[]{:S(2)}) copy-start(f32[64,512]{1,0:T(8,128)} %param.35) | copy-start | bytes 393220
  1151.8 47.5 %copy-start.34 = (f32[64,512]{1,0:T(8,128)S(1)}, f32[64,512]{1,0:T(8,128)}, u32[]{:S(2)}) copy-start(f32[64,512]{1,0:T(8,128)} %reduce-scatter.11.cloned.1.call-done) | copy-start | bytes 393220
  1155.5 45.5 %copy-start.32 = (f32[16,2048]{1,0:T(8,128)S(1)}, f32[16,2048]{1,0:T(8,128)}, u32[]{:S(2)}) copy-start(f32[16,2048]{1,0:T(8,128)} %param.32) | copy-start | bytes 393220
  1155.5 45.5 %copy-start.33 = (f32[16,2048]{1,0:T(8,128)S(1)}, f32[16,2048]{1,0:T(8,128)}, u32[]{:S(2)}) copy-start(f32[16,2048]{1,0:T(8,128)} %reduce-scatter.9.cloned.1.call-done) | copy-start | bytes 393220
  1155.5 45.5 %copy-start.37 = (f32[16,2048]{1,0:T(8,128)S(1)}, f32[16,2048]{1,0:T(8,128)}, u32[]{:S(2)}) copy-start(f32[16,2048]{1,0:T(8,128)} %param.33) | copy-start | bytes 393220
  1155.5 45.5 %copy-start.38 = (f32[16,2048]{1,0:T(8,128)S(1)}, f32[16,2048]{1,0:T(8,128)}, u32[]{:S(2)}) copy-start(f32[16,2048]{1,0:T(8,128)} %param.34) | copy-start | bytes 393220
Sparse Core Ops, SparseCore 0:
  11.5 59.1 all-gather.7
  74.1 52.4 all-gather.5
  130.1 55.1 all-gather.9
  188.6 55.0 all-gather.11
  448.9 134.4 reduce-scatter.12
  588.8 138.3 all-reduce.4
  729.5 137.3 reduce-scatter.6
  869.1 138.3 reduce-scatter.8
  1009.8 138.3 reduce-scatter.10
where the time goes:
time: 1210 us
  waiting for transfers between devices  711 us (59%)
  matrix products  237 us (20%)
  blocking collectives  158 us (13%)
  other arithmetic  47.2 us (4%)
  local copies, waits for them, and re-layouts  34.6 us (3%)
  between operations  20.6 us (2%)
    unnamed x11, waiting for transfers between devices  206 us
    reduce_scatter x1, waiting for transfers between devices, body(): lax.psum_scatter(grad_w_out, ('dp', 'inner'), scatter_dimension=0, tiled=...  139 us
    reduce_scatter x1, waiting for transfers between devices, body(): lax.psum_scatter(grad_w_in, ('dp', 'inner'), scatter_dimension=0, tiled=T...  138 us
    reduce_scatter x1, waiting for transfers between devices, body(): lax.psum_scatter(grad_gates, ('dp', 'inner'), scatter_dimension=1, tiled=...  137 us
    unnamed x2, blocking collectives  80.6 us
    dot_general x2, matrix products, attend_back(): jnp.einsum('hqk,khe->qhe', grad_raw, key_heads, preferred_element_type=jn...  66.9 us
    dot_general x2, matrix products, attend_back(): jnp.einsum('hqk,qhe->khe', grad_raw, query_part, preferred_element_type=j...  62.9 us
    all_gather x1, waiting for transfers between devices, fetch(): lax.all_gather(low_out, ('dp', 'inner'), axis=0, tiled=True)  51.2 us
  transfers between devices with their start and end apart: 9, of which 7 were waited for; matrix products, arithmetic and copies ran while one was open for 8% of the time, Pallas kernels for 0%

commit v1 on v0

--- a/solution.py
+++ b/solution.py
@@ -1,8 +1,10 @@
+import functools
 import jax
 import jax.numpy as jnp
 from jax import lax
 from jax.sharding import PartitionSpec as P
 
+AXES = ("dp", "inner")
 HEADS = 8
 HEAD = 64
 STEP = 10
@@ -36,18 +38,87 @@
     )
 
 
-def fetch(shards):
-    low_attn, low_gate, low_in, low_out, low_vec, low_shift = [
-        element.astype(jnp.bfloat16) for element in shards
-    ]
-    return (
-        lax.all_gather(low_attn, ("dp", "inner"), axis=1, tiled=True),
-        lax.all_gather(low_gate, ("dp", "inner"), axis=1, tiled=True),
-        lax.all_gather(low_in, ("dp", "inner"), axis=0, tiled=True),
-        lax.all_gather(low_out, ("dp", "inner"), axis=0, tiled=True),
-        lax.all_gather(low_vec, ("dp", "inner"), axis=1, tiled=True),
-        lax.all_gather(low_shift, ("dp", "inner"), axis=0, tiled=True),
-    )
+def bit_groups(sizes):
+    dp_bits = sizes["dp"].bit_length() - 1
+    inner_bits = sizes["inner"].bit_length() - 1
+    y_bits = dp_bits // 2
+    plane_bits = (inner_bits - 1) + y_bits
+    return (1, plane_bits, dp_bits - y_bits)
+
+
+def swap_with(array, offset, count):
+    return lax.ppermute(array, AXES, [(source, source ^ offset) for source in range(count)])
+
+
+def gather_chunk(shard, groups):
+    count = 2 ** sum(groups)
+    full = shard[None]
+    low_bits = groups[0] + groups[1]
+    for first_bit, bits in ((low_bits, groups[2]), (groups[0], groups[1]), (0, groups[0])):
+        parts = [full] + [
+            swap_with(full, offset << first_bit, count) for offset in range(1, 2**bits)
+        ]
+        full = jnp.stack(parts, 1)
+        full = full.reshape((-1,) + shard.shape)
+    return full
+
+
+def reduce_chunk(blocks, groups):
+    count = 2 ** sum(groups)
+    first_bit = 0
+    current = blocks
+    for bits in groups:
+        split = current.reshape((-1, 2**bits) + blocks.shape[1:])
+        total = split[:, 0].astype(jnp.float32)
+        for offset in range(1, 2**bits):
+            sent = split[:, offset].astype(jnp.bfloat16)
+            total = total + swap_with(sent, offset << first_bit, count).astype(jnp.float32)
+        first_bit += bits
+        current = total
+    return current[0]
+
+
+def sum_all(value, groups):
+    count = 2 ** sum(groups)
+    first_bit = 0
+    for bits in groups:
+        value = sum(
+            [value] + [swap_with(value, offset << first_bit, count) for offset in range(1, 2**bits)]
+        )
+        first_bit += bits
+    return value
+
+
+def pack(arrays, count):
+    attn, gate, w_in, w_out, vec, bias = arrays
+    width = 512
+    step = attn.shape[1] // count
+    parts = []
+    for matrix in [attn[0], attn[1], attn[2], gate[0], attn[3], gate[1]]:
+        parts.append(matrix.reshape(count, step, width))
+    for column in range(4):
+        parts.append(w_in[:, column * width : (column + 1) * width].reshape(count, step, width))
+    parts.append(w_out.reshape(count, 4 * step, width))
+    small = jnp.concatenate(
+        [vec.reshape(7, count, step).transpose(1, 0, 2).reshape(count, 7 * step), bias.reshape(count, 4 * step)], 1
+    )
+    small = jnp.pad(small, ((0, 0), (0, width - small.shape[1])))
+    parts.append(small[:, None])
+    return jnp.concatenate([part.astype(jnp.bfloat16) for part in parts], 1)
+
+
+def unpack(rows, count):
+    width = 512
+    step = (rows.shape[1] - 1) // 14
+    pieces = [rows[:, step * index : step * (index + 1)].reshape(count * step, width) for index in range(10)]
+    attn = jnp.stack([pieces[0], pieces[1], pieces[2], pieces[4]])
+    gate = jnp.stack([pieces[3], pieces[5]])
+    w_in = jnp.concatenate(pieces[6:10], 1)
+    w_out = rows[:, 10 * step : 14 * step].reshape(count * step * 4, width)
+    small = rows[:, 14 * step]
+    vec = small[:, : 7 * step].reshape(count, 7, step).transpose(1, 0, 2).reshape(7, count * step)
+    bias = small[:, 7 * step : 11 * step].reshape(-1)
+    return (attn, gate, w_in, w_out, vec, bias)
 
 
 def score_block(queries, key_heads, segments, positions, first_row, block_size):
@@ -169,6 +240,7 @@
 
 
 def body(
+    groups,
     tokens,
     segments,
     positions,
@@ -193,7 +265,12 @@
     bias_v,
 ):
     shards = (attn_weight, gate_weight, in_weight, out_weight, norm_params, in_bias)
-    weights = fetch(shards)
+    count = 2 ** sum(groups)
+    own = lax.axis_index(AXES)
+    order = jnp.arange(count) ^ own
+    shard_rows = pack(shards, 1)[0]
+    gathered = gather_chunk(shard_rows, groups)
+    weights = unpack(jnp.take(gathered, order, axis=0), count)
     vectors = weights[4].astype(jnp.float32)
     inputs = tokens.astype(jnp.float32)
     normed_full, unit_one, scale_one = normalize_parts(inputs, vectors[0], vectors[1])
@@ -210,9 +287,6 @@
         jnp.dot(normed_two, weights[1][1], preferred_element_type=jnp.float32) + vectors[5]
     )
     layer_out = (ffn_gate * branch + (1.0 - ffn_gate) * middle).astype(jnp.bfloat16)
-    weights = fetch(shards)
-    triple, mixed_heads, log_total, attended = attn_branch(weights, normed, segments, positions)
-    hidden, active, branch = ffn_branch(weights, normed_two)
     grad_out = cotangent.astype(jnp.float32)
     grad_branch = grad_out * ffn_gate
     grad_fgate = grad_out * (branch - middle) * ffn_gate * (1.0 - ffn_gate)
@@ -276,16 +350,11 @@
         ]
     )
     grad_bias = jnp.sum(grad_hidden, 0)
-    owned = (
-        lax.psum_scatter(grad_attn, ("dp", "inner"), scatter_dimension=1, tiled=True),
-        lax.psum_scatter(grad_gates, ("dp", "inner"), scatter_dimension=1, tiled=True),
-        lax.psum_scatter(grad_w_in, ("dp", "inner"), scatter_dimension=0, tiled=True),
-        lax.psum_scatter(grad_w_out, ("dp", "inner"), scatter_dimension=0, tiled=True),
-        lax.psum_scatter(grad_vectors, ("dp", "inner"), scatter_dimension=1, tiled=True),
-        lax.psum_scatter(grad_bias, ("dp", "inner"), scatter_dimension=0, tiled=True),
-    )
+    packed = pack((grad_attn, grad_gates, grad_w_in, grad_w_out, grad_vectors, grad_bias), count)
+    reduced = reduce_chunk(jnp.take(packed, order, axis=0), groups)
+    owned = unpack(reduced[None], 1)
     local_squares = sum((jnp.sum(element * element) for element in owned))
-    grad_norm = jnp.sqrt(lax.psum(local_squares, ("dp", "inner")))
+    grad_norm = jnp.sqrt(sum_all(local_squares, groups))
     factor = jnp.minimum(1.0, clip_norm / (grad_norm + 1e-06))
     states = (
         (attn_weight, attn_m, attn_v),
@@ -327,7 +396,7 @@
 
 def solution(mesh):
     return jax.shard_map(
-        body,
+        functools.partial(body, bit_groups(mesh.shape)),
         mesh=mesh,
         in_specs=(
             P(("dp", "inner"), None),

time: 1210 us -> 530 us (0.44)
  waiting for transfers between devices: 711 us -> 128 us
  blocking collectives: 158 us -> 0 us
  local copies, waits for them, and re-layouts: 34.6 us -> 81.5 us
  starting transfers between devices: 0.55 us -> 33.4 us
    reduce_scatter x3 -> x0, waiting for transfers between devices: 414 us -> none  [the longest x1 139 us: body(): lax.psum_scatter(grad_w_out, ('dp', 'inner'), scatter_dimension=0, tiled=...]
    unnamed x11 -> x0, waiting for transfers between devices: 206 us -> none
    ppermute x0 -> x21, waiting for transfers between devices: none -> 128 us  [swap_with(): lax.ppermute(array, AXES, [(source, source ^ offset) for source in range(...]
    all_gather x4 -> x0, waiting for transfers between devices: 92 us -> none  [the longest x1 51.2 us: fetch(): lax.all_gather(low_out, ('dp', 'inner'), axis=0, tiled=True)]
    unnamed x2 -> x0, blocking collectives: 80.6 us -> none
    all_gather x1 -> x0, blocking collectives: 40.4 us -> none  [fetch(): lax.all_gather(low_vec, ('dp', 'inner'), axis=1, tiled=True)]
    psum x1 -> x0, blocking collectives: 36.9 us -> none  [body(): grad_norm = jnp.sqrt(lax.psum(local_squares, ('dp', 'inner')))]
    ppermute x0 -> x21, starting transfers between devices: none -> 33.4 us  [swap_with(): lax.ppermute(array, AXES, [(source, source ^ offset) for source in range(...]
  transfers between devices with their start and end apart: 9 -> 21, of which waited for: 7 -> 14; matrix products, arithmetic and copies ran while one was open for 8% -> 1% of each run, Pallas kernels for 0% -> 0%
where the time goes in v1:
time: 530 us; the launch traced here: 525 us
  matrix products  226 us (43%)
  waiting for transfers between devices  128 us (24%)
  local copies, waits for them, and re-layouts  81.5 us (15%)
  other arithmetic  44.2 us (8%)
  starting transfers between devices  33.4 us (6%)
  between operations  11.5 us (2%)
    ppermute x21, waiting for transfers between devices, swap_with(): lax.ppermute(array, AXES, [(source, source ^ offset) for source in range(...  128 us
    dot_general x2, matrix products, attend_back(): jnp.einsum('hqk,khe->qhe', grad_raw, key_heads, preferred_element_type=jn...  67.6 us
    dot_general x2, matrix products, attend_back(): jnp.einsum('hqk,qhe->khe', grad_raw, query_part, preferred_element_type=j...  62.3 us
    ppermute x21, starting transfers between devices, swap_with(): lax.ppermute(array, AXES, [(source, source ^ offset) for source in range(...  33.4 us
    unnamed x184, local copies, waits for them, and re-layouts  23.9 us
    dot_general x2, matrix products, attend_back(): jnp.einsum('qhe,khe->hqk', grad_part, value_heads, preferred_element_type...  17.7 us
    dot_general x2, matrix products, attend_back(): jnp.einsum('hqk,qhe->khe', attn_probs.astype(jnp.bfloat16), grad_part, pr...  11.2 us
  transfers between devices with their start and end apart: 21, of which 14 were waited for; matrix products, arithmetic and copies ran while one was open for 1% of the time, Pallas kernels for 0%

profile of v1, /device:TPU:0, one launch (start us, length us, event | category | flops | bytes accessed | tf_op | source)
XLA Modules:
  0.0 525.1 jit_solution(1663387533652871507)
XLA Ops:
  5.9 5.1 collective-permute-start.2
  11.6 6.1 %collective-permute-done.2 = bf16[1,225,512]{2,1,0:T(8,128)(2,1)S(1)} collective-permute-done((bf16[1,225,512]{2,1,0:T(8,128)(2,1)S(1)}, bf16[1,225,512]{2,1,0:T(8,128)(2,1)S(1)}, u32[]{:S(2)}, u32[]{:S(2)}) %collective-permute-start.2) | collective-permute-done | bytes 230432 | tf_op jit(solution)/shard_map/ppermute | solution.py:50
  17.7 13.4 %collective-permute-done.1 = bf16[1,225,512]{2,1,0:T(8,128)(2,1)S(1)} collective-permute-done((bf16[1,225,512]{2,1,0:T(8,128)(2,1)S(1)}, bf16[1,225,512]{2,1,0:T(8,128)(2,1)S(1)}, u32[]{:S(2)}, u32[]{:S(2)}) %collective-permute-start.1) | collective-permute-done | bytes 230432 | tf_op jit(solution)/shard_map/ppermute | solution.py:50
  31.8 2.5 collective-permute-start.5
  35.4 20.8 %collective-permute-done.5 = bf16[4,225,512]{2,0,1:T(4,128)(2,1)S(1)} collective-permute-done((bf16[4,225,512]{2,0,1:T(4,128)(2,1)S(1)}, bf16[4,225,512]{2,0,1:T(4,128)(2,1)S(1)}, u32[]{:S(2)}, u32[]{:S(2)}) %collective-permute-start.5) | collective-permute-done | bytes 921632 | tf_op jit(solution)/shard_map/ppermute | solution.py:50
  56.3 17.7 %collective-permute-done.4 = bf16[4,225,512]{2,0,1:T(4,128)(2,1)S(1)} collective-permute-done((bf16[4,225,512]{2,0,1:T(4,128)(2,1)S(1)}, bf16[4,225,512]{2,0,1:T(4,128)(2,1)S(1)}, u32[]{:S(2)}, u32[]{:S(2)}) %collective-permute-start.4) | collective-permute-done | bytes 921632 | tf_op jit(solution)/shard_map/ppermute | solution.py:50
  75.4 3.1 copy.141
  79.3 2.0 compare_and_fusion.1
  81.3 3.9 collective-permute-done.6
  85.2 5.9 %copy.189 = bf16[16,225,512]{2,1,0:T(8,128)(2,1)} copy(bf16[16,225,512]{2,0,1:T(8,128)(2,1)} %collective-permute-done.6) | data formatting | bytes 7372800 | tf_op jit(solution)/shard_map/ppermute | solution.py:50
  91.2 2.7 pad_maximum_fusion
  93.9 3.8 copy.143
  97.7 7.3 %gather_fusion = bf16[32,225,512]{2,1,0:T(8,128)(2,1)} fusion(bf16[32,225,512]{2,1,0:T(8,128)(2,1)} %bitcast.224, s32[1024]{0:T(1024)S(1)} %pad_clamp_fusion), kind=kCustom, calls=%fused_computation.clone | custom fusion | bytes 14745728 | tf_op jit(solution)/shard_map/jit(_take)/gather | solution.py:273
  105.0 3.9 broadcast_select_fusion.1
  109.0 3.0 copy-done.4
  112.2 3.1 slice.388
  115.3 4.4 fusion.157
  121.6 3.3 convert_bitcast_fusion
  126.0 3.2 fusion.166
  129.2 4.0 fusion.9
  135.0 3.8 fusion.86
  138.8 3.2 fusion.167
  142.0 3.5 fusion.8
  145.6 2.2 copy-done.1
  147.8 4.5 fusion.87
  154.9 3.3 fusion.155
  158.7 2.4 fusion.100
  161.2 2.4 fusion.89
  163.6 3.1 fusion.150
  166.7 3.8 convolution_convert_fusion
  170.5 4.4 fusion.168
  175.0 4.7 fusion.67
  179.7 4.0 convolution_convert_fusion.1
  186.9 2.3 fusion.152
  195.2 8.1 %fusion.169 = f32[8,512,1024]{2,1,0:T(8,128)} fusion(bf16[512,8,64]{0,2,1:T(8,128)(2,1)S(1)} %bitcast.234, bf16[1024,8,64]{0,2,1:T(8,128)(2,1)S(1)} %bitcast.227), kind=kOutput, calls=%fused_computation.287 | convolution fusion | flops 536870912 | bytes 18350080 | tf_op jit(solution)/shard_map/qhe,khe->hqk/dot_general | solution.py:180
  203.3 30.2 %fusion.83 = bf16[8,64,512]{2,1,0:T(8,128)(2,1)} fusion(bf16[1024,8,64]{0,2,1:T(8,128)(2,1)} %bitcast.232, f32[8,512,1024]{2,1,0:T(8,128)} %fusion.169, f32[8,512,1024]{2,1,0:T(8,128)} %copy-done.1, f32[8,512]{1,0:T(8,128)S(1)} %log_add_fusion.1), kind=kOutput, calls=%fused_computation.116 | convolution fusion | flops 566498304 | bytes 35143680 | tf_op jit(solution)/shard_map/hqk,khe->qhe/dot_general | solution.py:186
  233.5 30.9 %fusion.13 = f32[8,64,1024]{2,1,0:T(8,128)} fusion(bf16[512,8,64]{0,2,1:T(8,128)(2,1)} %bitcast.253, f32[8,512,1024]{2,1,0:T(8,128)} %fusion.169, f32[8,512,1024]{2,1,0:T(8,128)} %copy-done.1, f32[8,512]{1,0:T(8,128)S(1)} %log_add_fusion.1), kind=kOutput, calls=%fused_computation.22 | convolution fusion | flops 566236160 | bytes 36192256 | tf_op jit(solution)/shard_map/hqk,qhe->khe/dot_general | solution.py:190
  264.4 9.5 %fusion.170 = f32[8,512,1024]{2,1,0:T(8,128)} fusion(bf16[512,8,64]{0,2,1:T(8,128)(2,1)} %bitcast.236, bf16[1024,8,64]{0,2,1:T(8,128)(2,1)S(1)} %bitcast.228), kind=kOutput, calls=%fused_computation.288 | convolution fusion | flops 536870912 | bytes 18350080 | tf_op jit(solution)/shard_map/qhe,khe->hqk/dot_general | solution.py:180
  274.0 7.4 %fusion.24 = f32[8,64,1024]{2,1,0:T(8,128)S(1)} fusion(bf16[512,8,64]{0,2,1:T(8,128)(2,1)S(1)} %bitcast.237, f32[8,512,1024]{2,1,0:T(8,128)} %copy-done, f32[8,512]{1,0:T(8,128)S(1)} %log_add_fusion), kind=kOutput, calls=%fused_computation.26 | convolution fusion | flops 545259520 | bytes 19415040 | tf_op jit(solution)/shard_map/hqk,qhe->khe/dot_general | solution.py:193
  281.4 3.8 add_convert_fusion
  285.2 2.4 copy.158
  287.6 2.1 copy.155
  289.7 37.4 %fusion.80 = bf16[8,64,512]{2,1,0:T(8,128)(2,1)} fusion(bf16[1024,8,64]{0,2,1:T(8,128)(2,1)S(1)} %bitcast.233, f32[8,512,1024]{2,1,0:T(8,128)} %fusion.170, f32[8,512,1024]{2,1,0:T(8,128)} %copy-done, f32[8,512]{1,0:T(8,128)S(1)} %log_add_fusion), kind=kOutput, calls=%fused_computation.115 | convolution fusion | flops 566498304 | bytes 35143680 | tf_op jit(solution)/shard_map/hqk,khe->qhe/dot_general | solution.py:186
  327.1 31.3 %add_convert_fusion.1 = bf16[8,64,1024]{2,1,0:T(8,128)(2,1)} fusion(f32[8,64,1024]{2,1,0:T(8,128)} %fusion.13, bf16[512,8,64]{0,2,1:T(8,128)(2,1)} %bitcast.251, f32[8,512,1024]{2,1,0:T(8,128)} %fusion.170, f32[8,512,1024]{2,1,0:T(8,128)} %copy-done, f32[8,512]{1,0:T(8,128)S(1)} %log_add_fusion), kind=kOutput, calls=%fused_computation.87 | convolution fusion | flops 567284736 | bytes 37240832 | tf_op jit(solution)/shard_map/hqk,qhe->khe/dot_general | solution.py:190
  359.8 2.4 copy.157
  362.3 5.3 %fusion.88 = f32[1024,512,1]{1,0,2:T(8,128)} fusion(bf16[1,1024,512]{2,1,0:T(8,128)(2,1)} %copy.158, bf16[1,1024,512]{2,1,0:T(8,128)(2,1)} %copy.157, bf16[1,1024,512]{2,1,0:T(8,128)(2,1)S(1)} %maximum_bitcast_fusion, bf16[1,512,512]{1,2,0:T(8,128)(2,1)} %copy.150, bf16[1,512,512]{1,2,0:T(8,128)(2,1)} %copy-done.44, bf16[1,512,512]{1,2,0:T(8,128)(2,1)} %copy-done.45), kind=kOutput, calls=%fused_computation.122 | convolution fusion | flops 1615331328 | bytes 6815744 | tf_op jit(solution)/shard_map/jte,jde->td/dot_general | solution.py:329
  367.7 3.2 fusion.77
  371.1 2.9 fusion.160
  374.4 3.3 convolution_convert_fusion.6
  377.7 2.5 fusion.57
  381.9 2.1 constant_dynamic-update-slice_fusion.28
  396.2 7.4 %gather_fusion.1 = bf16[32,225,512]{2,1,0:T(8,128)(2,1)} fusion(bf16[32,225,512]{2,1,0:T(8,128)(2,1)} %copy_dynamic-update-slice_fusion, s32[1024]{0:T(1024)} %copy-done.61), kind=kCustom, calls=%fused_computation.1.clone | custom fusion | bytes 14745728 | tf_op jit(solution)/shard_map/jit(_take)/gather | solution.py:354
  403.6 3.9 broadcast_select_fusion
  409.3 6.3 %collective-permute-done.7 = bf16[16,225,512]{2,0,1:T(8,128)(2,1)S(1)} collective-permute-done((bf16[16,225,512]{2,0,1:T(8,128)(2,1)S(1)}, bf16[16,225,512]{2,0,1:T(8,128)(2,1)S(1)}, u32[]{:S(2)}, u32[]{:S(2)}) %collective-permute-start.7) | collective-permute-done | bytes 3686432 | tf_op jit(solution)/shard_map/ppermute | solution.py:50
  415.6 2.7 convert_add_fusion
  424.1 38.7 %collective-permute-done.9 = bf16[4,225,512]{2,0,1:T(4,128)(2,1)S(1)} collective-permute-done((bf16[4,225,512]{2,0,1:T(4,128)(2,1)S(1)}, bf16[4,225,512]{2,0,1:T(4,128)(2,1)S(1)}, u32[]{:S(2)}, u32[]{:S(2)}) %collective-permute-start.9) | collective-permute-done | bytes 921632 | tf_op jit(solution)/shard_map/ppermute | solution.py:50
  464.9 2.4 collective-permute-start.13
  470.4 5.7 %collective-permute-done.11 = bf16[1,225,512]{2,1,0:T(8,128)(2,1)S(1)} collective-permute-done((bf16[1,225,512]{2,1,0:T(8,128)(2,1)S(1)}, bf16[1,225,512]{2,1,0:T(8,128)(2,1)S(1)}, u32[]{:S(2)}, u32[]{:S(2)}) %collective-permute-start.11) | collective-permute-done | bytes 230432 | tf_op jit(solution)/shard_map/ppermute | solution.py:50
  476.1 2.9 collective-permute-done.13
  479.0 9.1 %collective-permute-done.12 = bf16[1,225,512]{2,1,0:T(8,128)(2,1)S(1)} collective-permute-done((bf16[1,225,512]{2,1,0:T(8,128)(2,1)S(1)}, bf16[1,225,512]{2,1,0:T(8,128)(2,1)S(1)}, u32[]{:S(2)}, u32[]{:S(2)}) %collective-permute-start.12) | collective-permute-done | bytes 230432 | tf_op jit(solution)/shard_map/ppermute | solution.py:50
  497.8 3.1 collective-permute-start.17
  501.0 2.5 collective-permute-start.16
  508.8 3.7 collective-permute-start.20
  513.8 3.4 collective-permute-start.18
  (315 shorter events, 70.0 us)
Async XLA Ops:
  5.9 11.9 %collective-permute-start.2 = (bf16[1,225,512]{2,1,0:T(8,128)(2,1)S(1)}, bf16[1,225,512]{2,1,0:T(8,128)(2,1)S(1)}, u32[]{:S(2)}, u32[]{:S(2)}) collective-permute-start(bf16[1,225,512]{2,1,0:T(8,128)(2,1)S(1)} %constant_dynamic-update-slice_fusion), channel_id=1, source_target_pairs={{0,24},{1,25},{2,26},{3,27},{4,28},{5,29},{6,30},{7,31},{8,16},{9,... | collective-permute-start | bytes 691208 | tf_op jit(solution)/shard_map/ppermute | solution.py:50
  11.0 20.2 %collective-permute-start.1 = (bf16[1,225,512]{2,1,0:T(8,128)(2,1)S(1)}, bf16[1,225,512]{2,1,0:T(8,128)(2,1)S(1)}, u32[]{:S(2)}, u32[]{:S(2)}) collective-permute-start(bf16[1,225,512]{2,1,0:T(8,128)(2,1)S(1)} %constant_dynamic-update-slice_fusion), channel_id=1, source_target_pairs={{0,16},{1,17},{2,18},{3,19},{4,20},{5,21},{6,22},{7,23},{8,24},{9,... | collective-permute-start | bytes 691208 | tf_op jit(solution)/shard_map/ppermute | solution.py:50
  11.0 20.2 %collective-permute-start = (bf16[1,225,512]{2,1,0:T(8,128)(2,1)S(1)}, bf16[1,225,512]{2,1,0:T(8,128)(2,1)S(1)}, u32[]{:S(2)}, u32[]{:S(2)}) collective-permute-start(bf16[1,225,512]{2,1,0:T(8,128)(2,1)S(1)} %constant_dynamic-update-slice_fusion), channel_id=1, source_target_pairs={{0,8},{1,9},{2,10},{3,11},{4,12},{5,13},{6,14},{7,15},{8,0},{9,1},... | collective-permute-start | bytes 691208 | tf_op jit(solution)/shard_map/ppermute | solution.py:50
  31.8 24.3 %collective-permute-start.5 = (bf16[4,225,512]{2,0,1:T(4,128)(2,1)S(1)}, bf16[4,225,512]{2,0,1:T(4,128)(2,1)S(1)}, u32[]{:S(2)}, u32[]{:S(2)}) collective-permute-start(bf16[4,225,512]{2,0,1:T(4,128)(2,1)S(1)} %copy.133), channel_id=1, source_target_pairs={{0,6},{1,7},{2,4},{3,5},{4,2},{5,3},{6,0},{7,1},{8,14},{9,15},{10,... | collective-permute-start | bytes 2764808 | tf_op jit(solution)/shard_map/ppermute | solution.py:50
  34.3 39.7 %collective-permute-start.4 = (bf16[4,225,512]{2,0,1:T(4,128)(2,1)S(1)}, bf16[4,225,512]{2,0,1:T(4,128)(2,1)S(1)}, u32[]{:S(2)}, u32[]{:S(2)}) collective-permute-start(bf16[4,225,512]{2,0,1:T(4,128)(2,1)S(1)} %copy.133), channel_id=1, source_target_pairs={{0,4},{1,5},{2,6},{3,7},{4,0},{5,1},{6,2},{7,3},{8,12},{9,13},{10,... | collective-permute-start | bytes 2764808 | tf_op jit(solution)/shard_map/ppermute | solution.py:50
  34.8 39.4 %collective-permute-start.3 = (bf16[4,225,512]{2,0,1:T(4,128)(2,1)S(1)}, bf16[4,225,512]{2,0,1:T(4,128)(2,1)S(1)}, u32[]{:S(2)}, u32[]{:S(2)}) collective-permute-start(bf16[4,225,512]{2,0,1:T(4,128)(2,1)S(1)} %copy.133), channel_id=1, source_target_pairs={{0,2},{1,3},{2,0},{3,1},{4,6},{5,7},{6,4},{7,5},{8,10},{9,11},{10,... | collective-permute-start | bytes 2764808 | tf_op jit(solution)/shard_map/ppermute | solution.py:50
  78.4 6.8 %collective-permute-start.6 = (bf16[16,225,512]{2,0,1:T(8,128)(2,1)}, bf16[16,225,512]{2,0,1:T(8,128)(2,1)}, u32[]{:S(2)}, u32[]{:S(2)}) collective-permute-start(bf16[16,225,512]{2,0,1:T(8,128)(2,1)} %copy.141), channel_id=1, source_target_pairs={{0,1},{1,0},{2,3},{3,2},{4,5},{5,4},{6,7},{7,6},{8,9},{9,8},{10,11... | collective-permute-start | bytes 11059208 | tf_op jit(solution)/shard_map/ppermute | solution.py:50
  78.5 26.5 %copy-start.64 = (pred[32]{0:T(512)(128)(4,1)}, pred[32]{0:T(512)(128)(4,1)S(1)}, u32[]{:S(2)}) copy-start(pred[32]{0:T(512)(128)(4,1)S(1)} %compare_and_fusion.2) | copy-start | bytes 100
  78.5 19.2 %copy-start.61 = (s32[1024]{0:T(1024)}, s32[1024]{0:T(1024)S(1)}, u32[]{:S(2)}) copy-start(s32[1024]{0:T(1024)S(1)} %pad_clamp_fusion) | copy-start | bytes 12292
  81.3 9.8 %copy-start.3 = (bf16[4,4,225,512]{3,2,1,0:T(8,128)(2,1)S(1)}, bf16[4,4,225,512]{3,2,1,0:T(8,128)(2,1)}, u32[]{:S(2)}) copy-start(bf16[4,4,225,512]{3,2,1,0:T(8,128)(2,1)} %copy-done.2) | copy-start | bytes 11059204
  119.8 33.3 %copy-start.35 = (bf16[32,16,512]{2,1,0:T(8,128)(2,1)}, bf16[32,16,512]{2,1,0:T(8,128)(2,1)S(1)}, u32[]{:S(2)}) copy-start(bf16[32,16,512]{2,1,0:T(8,128)(2,1)S(1)} %get-tuple-element.62) | copy-start | bytes 1572868
  124.9 13.9 %copy-start.23 = (bf16[1,512,512]{1,2,0:T(8,128)(2,1)}, bf16[1,512,512]{1,2,0:T(8,128)(2,1)S(1)}, u32[]{:S(2)}) copy-start(bf16[1,512,512]{1,2,0:T(8,128)(2,1)S(1)} %get-tuple-element.72) | copy-start | bytes 1572868
  125.1 13.7 %copy-start.11 = (bf16[1,1024,512]{1,2,0:T(8,128)(2,1)}, bf16[1,1024,512]{1,2,0:T(8,128)(2,1)S(1)}, u32[]{:S(2)}) copy-start(bf16[1,1024,512]{1,2,0:T(8,128)(2,1)S(1)} %get-tuple-element.74) | copy-start | bytes 3145732
  129.2 5.8 %copy-start = (f32[8,512,1024]{2,1,0:T(8,128)}, f32[8,512,1024]{2,1,0:T(8,128)S(1)}, u32[]{:S(2)}) copy-start(f32[8,512,1024]{2,1,0:T(8,128)S(1)} %get-tuple-element.113) | copy-start | bytes 50331652
  138.8 14.3 %copy-start.69 = (bf16[8,64,512]{2,1,0:T(8,128)(2,1)}, bf16[8,64,512]{2,1,0:T(8,128)(2,1)S(1)}, u32[]{:S(2)}) copy-start(bf16[8,64,512]{2,1,0:T(8,128)(2,1)S(1)} %fusion.86) | copy-start | bytes 1572868
  142.0 5.7 %copy-start.1 = (f32[8,512,1024]{2,1,0:T(8,128)}, f32[8,512,1024]{2,1,0:T(8,128)S(1)}, u32[]{:S(2)}) copy-start(f32[8,512,1024]{2,1,0:T(8,128)S(1)} %get-tuple-element.115) | copy-start | bytes 50331652
  264.4 9.6 %copy-start.15 = (bf16[512,512]{0,1:T(8,128)(2,1)S(1)}, bf16[512,512]{0,1:T(8,128)(2,1)}, u32[]{:S(2)}) copy-start(bf16[512,512]{0,1:T(8,128)(2,1)} %get-tuple-element.84) | copy-start | bytes 1572868
  264.4 17.0 %slice-start = ((s8[16777216]{0:T(1024)(128)(4,1)}), s8[4194304]{0:T(1024)(128)(4,1)S(1)}, s32[]{:S(2)}) async-start(s8[16777216]{0:T(1024)(128)(4,1)} %bitcast.216), calls=%async_computation | async-start | bytes 8388608
  264.4 17.0 %slice-start.1 = ((s8[16777216]{0:T(1024)(128)(4,1)}), s8[4194304]{0:T(1024)(128)(4,1)S(1)}, s32[]{:S(2)}) async-start(s8[16777216]{0:T(1024)(128)(4,1)} %bitcast.216), calls=%async_computation.1 | async-start | bytes 8388608
  264.4 17.0 %slice-start.2 = ((s8[16777216]{0:T(1024)(128)(4,1)}), s8[4194304]{0:T(1024)(128)(4,1)S(1)}, s32[]{:S(2)}) async-start(s8[16777216]{0:T(1024)(128)(4,1)} %bitcast.216), calls=%async_computation.2 | async-start | bytes 8388608
  274.0 7.4 %slice-start.3 = ((s8[16777216]{0:T(1024)(128)(4,1)}), s8[4194304]{0:T(1024)(128)(4,1)S(1)}, s32[]{:S(2)}) async-start(s8[16777216]{0:T(1024)(128)(4,1)} %bitcast.216), calls=%async_computation.3 | async-start | bytes 8388608
  274.0 7.5 %copy-start.14 = (bf16[512,512]{0,1:T(8,128)(2,1)S(1)}, bf16[512,512]{0,1:T(8,128)(2,1)}, u32[]{:S(2)}) copy-start(bf16[512,512]{0,1:T(8,128)(2,1)} %copy-done.13) | copy-start | bytes 1572868
  362.3 5.4 %copy-start.10 = (bf16[1024,512]{1,0:T(8,128)(2,1)S(1)}, bf16[1024,512]{1,0:T(8,128)(2,1)}, u32[]{:S(2)}) copy-start(bf16[1024,512]{1,0:T(8,128)(2,1)} %param.24) | copy-start | bytes 3145732
  381.8 6.1 %copy-start.48 = (bf16[512,512]{1,0:T(8,128)(2,1)S(1)}, bf16[512,512]{1,0:T(8,128)(2,1)}, u32[]{:S(2)}) copy-start(bf16[512,512]{1,0:T(8,128)(2,1)} %convolution_convert_fusion.6) | copy-start | bytes 1572868
  381.8 7.0 %copy-start.47 = (bf16[512,512]{1,0:T(8,128)(2,1)S(1)}, bf16[512,512]{1,0:T(8,128)(2,1)}, u32[]{:S(2)}) copy-start(bf16[512,512]{1,0:T(8,128)(2,1)} %convolution_convert_fusion.5) | copy-start | bytes 1572868
  381.8 7.9 %copy-start.46 = (bf16[512,512]{1,0:T(8,128)(2,1)S(1)}, bf16[512,512]{1,0:T(8,128)(2,1)}, u32[]{:S(2)}) copy-start(bf16[512,512]{1,0:T(8,128)(2,1)} %convolution_convert_fusion.4) | copy-start | bytes 1572868
  381.9 8.7 %copy-start.28 = (bf16[512,512]{1,0:T(8,128)(2,1)S(1)}, bf16[512,512]{1,0:T(8,128)(2,1)}, u32[]{:S(2)}) copy-start(bf16[512,512]{1,0:T(8,128)(2,1)} %get-tuple-element.79) | copy-start | bytes 1572868
  384.0 7.4 %copy-start.27 = (bf16[512,512]{1,0:T(8,128)(2,1)S(1)}, bf16[512,512]{1,0:T(8,128)(2,1)}, u32[]{:S(2)}) copy-start(bf16[512,512]{1,0:T(8,128)(2,1)} %get-tuple-element.78) | copy-start | bytes 1572868
  386.0 6.3 %copy-start.26 = (bf16[512,512]{1,0:T(8,128)(2,1)S(1)}, bf16[512,512]{1,0:T(8,128)(2,1)}, u32[]{:S(2)}) copy-start(bf16[512,512]{1,0:T(8,128)(2,1)} %get-tuple-element.77) | copy-start | bytes 1572868
  396.2 7.4 %copy-start.65 = (pred[32]{0:T(512)(128)(4,1)S(1)}, pred[32]{0:T(512)(128)(4,1)}, u32[]{:S(2)}) copy-start(pred[32]{0:T(512)(128)(4,1)} %copy-done.64) | copy-start | bytes 100
  409.1 6.5 %collective-permute-start.7 = (bf16[16,225,512]{2,0,1:T(8,128)(2,1)S(1)}, bf16[16,225,512]{2,0,1:T(8,128)(2,1)S(1)}, u32[]{:S(2)}, u32[]{:S(2)}) collective-permute-start(bf16[16,225,512]{2,0,1:T(8,128)(2,1)S(1)} %copy.164), channel_id=1, source_target_pairs={{0,1},{1,0},{2,3},{3,2},{4,5},{5,4},{6,7},{7,6},{8,9},{9,8},{10,11... | collective-permute-start | bytes 11059208 | tf_op jit(solution)/shard_map/ppermute | solution.py:50
  420.6 42.3 %collective-permute-start.9 = (bf16[4,225,512]{2,0,1:T(4,128)(2,1)S(1)}, bf16[4,225,512]{2,0,1:T(4,128)(2,1)S(1)}, u32[]{:S(2)}, u32[]{:S(2)}) collective-permute-start(bf16[4,225,512]{2,0,1:T(4,128)(2,1)S(1)} %copy.168), channel_id=1, source_target_pairs={{0,4},{1,5},{2,6},{3,7},{4,0},{5,1},{6,2},{7,3},{8,12},{9,13},{10,... | collective-permute-start | bytes 2764808 | tf_op jit(solution)/shard_map/ppermute | solution.py:50
  422.2 40.7 %collective-permute-start.10 = (bf16[4,225,512]{2,0,1:T(4,128)(2,1)S(1)}, bf16[4,225,512]{2,0,1:T(4,128)(2,1)S(1)}, u32[]{:S(2)}, u32[]{:S(2)}) collective-permute-start(bf16[4,225,512]{2,0,1:T(4,128)(2,1)S(1)} %copy.170), channel_id=1, source_target_pairs={{0,6},{1,7},{2,4},{3,5},{4,2},{5,3},{6,0},{7,1},{8,14},{9,15},{10,... | collective-permute-start | bytes 2764808 | tf_op jit(solution)/shard_map/ppermute | solution.py:50
  423.6 40.5 %collective-permute-start.8 = (bf16[4,225,512]{2,0,1:T(4,128)(2,1)S(1)}, bf16[4,225,512]{2,0,1:T(4,128)(2,1)S(1)}, u32[]{:S(2)}, u32[]{:S(2)}) collective-permute-start(bf16[4,225,512]{2,0,1:T(4,128)(2,1)S(1)} %copy.166), channel_id=1, source_target_pairs={{0,2},{1,3},{2,0},{3,1},{4,6},{5,7},{6,4},{7,5},{8,10},{9,11},{10,... | collective-permute-start | bytes 2764808 | tf_op jit(solution)/shard_map/ppermute | solution.py:50
  424.1 44.2 %copy-start.6 = (f32[1024,512]{1,0:T(8,128)S(1)}, f32[1024,512]{1,0:T(8,128)}, u32[]{:S(2)}) copy-start(f32[1024,512]{1,0:T(8,128)} %copy-done.5) | copy-start | bytes 6291460
  424.1 44.2 %copy-start.16 = (f32[1024,512]{1,0:T(8,128)S(1)}, f32[1024,512]{1,0:T(8,128)}, u32[]{:S(2)}) copy-start(f32[1024,512]{1,0:T(8,128)} %get-tuple-element.119) | copy-start | bytes 6291460
  464.8 11.3 %collective-permute-start.11 = (bf16[1,225,512]{2,1,0:T(8,128)(2,1)S(1)}, bf16[1,225,512]{2,1,0:T(8,128)(2,1)S(1)}, u32[]{:S(2)}, u32[]{:S(2)}) collective-permute-start(bf16[1,225,512]{2,1,0:T(8,128)(2,1)S(1)} %get-tuple-element.85), channel_id=1, source_target_pairs={{0,8},{1,9},{2,10},{3,11},{4,12},{5,13},{6,14},{7,15},{8,0},{9,1},... | collective-permute-start | bytes 691208 | tf_op jit(solution)/shard_map/ppermute | solution.py:50
  464.9 14.1 %collective-permute-start.13 = (bf16[1,225,512]{2,1,0:T(8,128)(2,1)S(1)}, bf16[1,225,512]{2,1,0:T(8,128)(2,1)S(1)}, u32[]{:S(2)}, u32[]{:S(2)}) collective-permute-start(bf16[1,225,512]{2,1,0:T(8,128)(2,1)S(1)} %get-tuple-element.86), channel_id=1, source_target_pairs={{0,24},{1,25},{2,26},{3,27},{4,28},{5,29},{6,30},{7,31},{8,16},{9,... | collective-permute-start | bytes 691208 | tf_op jit(solution)/shard_map/ppermute | solution.py:50
  467.3 20.8 %collective-permute-start.12 = (bf16[1,225,512]{2,1,0:T(8,128)(2,1)S(1)}, bf16[1,225,512]{2,1,0:T(8,128)(2,1)S(1)}, u32[]{:S(2)}, u32[]{:S(2)}) collective-permute-start(bf16[1,225,512]{2,1,0:T(8,128)(2,1)S(1)} %get-tuple-element.87), channel_id=1, source_target_pairs={{0,16},{1,17},{2,18},{3,19},{4,20},{5,21},{6,22},{7,23},{8,24},{9,... | collective-permute-start | bytes 691208 | tf_op jit(solution)/shard_map/ppermute | solution.py:50
  468.4 51.0 %copy-start.41 = (f32[64,512]{1,0:T(8,128)S(1)}, f32[64,512]{1,0:T(8,128)}, u32[]{:S(2)}) copy-start(f32[64,512]{1,0:T(8,128)} %param.37) | copy-start | bytes 393220
  468.4 51.0 %copy-start.50 = (f32[64,512]{1,0:T(8,128)S(1)}, f32[64,512]{1,0:T(8,128)}, u32[]{:S(2)}) copy-start(f32[64,512]{1,0:T(8,128)} %param.38) | copy-start | bytes 393220
  468.4 51.0 %copy-start.51 = (f32[64,512]{1,0:T(8,128)S(1)}, f32[64,512]{1,0:T(8,128)}, u32[]{:S(2)}) copy-start(f32[64,512]{1,0:T(8,128)} %param.39) | copy-start | bytes 393220
  470.3 49.9 %copy-start.66 = (f32[64]{0:T(128)S(1)}, f32[64]{0:T(128)}, u32[]{:S(2)}) copy-start(f32[64]{0:T(128)} %param.43) | copy-start | bytes 772
  470.3 49.9 %copy-start.67 = (f32[64]{0:T(128)S(1)}, f32[64]{0:T(128)}, u32[]{:S(2)}) copy-start(f32[64]{0:T(128)} %param.44) | copy-start | bytes 772
  470.3 49.9 %copy-start.68 = (f32[64]{0:T(128)S(1)}, f32[64]{0:T(128)}, u32[]{:S(2)}) copy-start(f32[64]{0:T(128)} %param.45) | copy-start | bytes 772
  470.3 50.5 %copy-start.49 = (f32[2,16,512]{2,1,0:T(8,128)S(1)}, f32[2,16,512]{2,1,0:T(8,128)}, u32[]{:S(2)}) copy-start(f32[2,16,512]{2,1,0:T(8,128)} %param.31) | copy-start | bytes 196612
  470.3 50.5 %copy-start.56 = (f32[2,16,512]{2,1,0:T(8,128)S(1)}, f32[2,16,512]{2,1,0:T(8,128)}, u32[]{:S(2)}) copy-start(f32[2,16,512]{2,1,0:T(8,128)} %param.32) | copy-start | bytes 196612
  470.3 50.5 %copy-start.57 = (f32[2,16,512]{2,1,0:T(8,128)S(1)}, f32[2,16,512]{2,1,0:T(8,128)}, u32[]{:S(2)}) copy-start(f32[2,16,512]{2,1,0:T(8,128)} %param.33) | copy-start | bytes 196612
  470.3 51.2 %copy-start.42 = (f32[16,2048]{1,0:T(8,128)S(1)}, f32[16,2048]{1,0:T(8,128)}, u32[]{:S(2)}) copy-start(f32[16,2048]{1,0:T(8,128)} %param.34) | copy-start | bytes 393220
  470.3 51.2 %copy-start.52 = (f32[16,2048]{1,0:T(8,128)S(1)}, f32[16,2048]{1,0:T(8,128)}, u32[]{:S(2)}) copy-start(f32[16,2048]{1,0:T(8,128)} %param.35) | copy-start | bytes 393220
  470.3 51.2 %copy-start.53 = (f32[16,2048]{1,0:T(8,128)S(1)}, f32[16,2048]{1,0:T(8,128)}, u32[]{:S(2)}) copy-start(f32[16,2048]{1,0:T(8,128)} %param.36) | copy-start | bytes 393220
  470.3 52.0 %copy-start.43 = (f32[4,16,512]{2,1,0:T(8,128)S(1)}, f32[4,16,512]{2,1,0:T(8,128)}, u32[]{:S(2)}) copy-start(f32[4,16,512]{2,1,0:T(8,128)} %param.28) | copy-start | bytes 393220
  470.3 52.0 %copy-start.54 = (f32[4,16,512]{2,1,0:T(8,128)S(1)}, f32[4,16,512]{2,1,0:T(8,128)}, u32[]{:S(2)}) copy-start(f32[4,16,512]{2,1,0:T(8,128)} %param.29) | copy-start | bytes 393220
  470.4 52.0 %copy-start.55 = (f32[4,16,512]{2,1,0:T(8,128)S(1)}, f32[4,16,512]{2,1,0:T(8,128)}, u32[]{:S(2)}) copy-start(f32[4,16,512]{2,1,0:T(8,128)} %param.30) | copy-start | bytes 393220
  470.4 52.8 %copy-start.60 = (f32[7,16]{1,0:T(8,128)S(1)}, f32[7,16]{1,0:T(8,128)}, u32[]{:S(2)}) copy-start(f32[7,16]{1,0:T(8,128)} %param.40) | copy-start | bytes 1348
  470.4 52.8 %copy-start.62 = (f32[7,16]{1,0:T(8,128)S(1)}, f32[7,16]{1,0:T(8,128)}, u32[]{:S(2)}) copy-start(f32[7,16]{1,0:T(8,128)} %param.41) | copy-start | bytes 1348
  470.4 52.8 %copy-start.63 = (f32[7,16]{1,0:T(8,128)S(1)}, f32[7,16]{1,0:T(8,128)}, u32[]{:S(2)}) copy-start(f32[7,16]{1,0:T(8,128)} %param.42) | copy-start | bytes 1348
  495.9 1.4 collective-permute-start.14
  497.8 10.4 %collective-permute-start.17 = (f32[]{:T(128)}, f32[]{:T(128)}, u32[]{:S(2)}, u32[]{:S(2)}) collective-permute-start(f32[]{:T(128)} %add.332), channel_id=1, source_target_pairs={{0,6},{1,7},{2,4},{3,5},{4,2},{5,3},{6,0},{7,1},{8,14},{9,15},{10,... | collective-permute-start | bytes 20 | tf_op jit(solution)/shard_map/ppermute | solution.py:50
  501.0 6.6 %collective-permute-start.16 = (f32[]{:T(128)}, f32[]{:T(128)}, u32[]{:S(2)}, u32[]{:S(2)}) collective-permute-start(f32[]{:T(128)} %add.332), channel_id=1, source_target_pairs={{0,4},{1,5},{2,6},{3,7},{4,0},{5,1},{6,2},{7,3},{8,12},{9,13},{10,... | collective-permute-start | bytes 20 | tf_op jit(solution)/shard_map/ppermute | solution.py:50
  503.4 3.5 collective-permute-start.15
  508.8 9.8 %collective-permute-start.20 = (f32[]{:T(128)}, f32[]{:T(128)}, u32[]{:S(2)}, u32[]{:S(2)}) collective-permute-start(f32[]{:T(128)} %add.335), channel_id=1, source_target_pairs={{0,24},{1,25},{2,26},{3,27},{4,28},{5,29},{6,30},{7,31},{8,16},{9,... | collective-permute-start | bytes 20 | tf_op jit(solution)/shard_map/ppermute | solution.py:50
  512.5 5.5 %collective-permute-start.19 = (f32[]{:T(128)}, f32[]{:T(128)}, u32[]{:S(2)}, u32[]{:S(2)}) collective-permute-start(f32[]{:T(128)} %add.335), channel_id=1, source_target_pairs={{0,16},{1,17},{2,18},{3,19},{4,20},{5,21},{6,22},{7,23},{8,24},{9,... | collective-permute-start | bytes 20 | tf_op jit(solution)/shard_map/ppermute | solution.py:50
  513.8 3.6 collective-permute-start.18
  (35 other events, 114.3 us)
